TPU v7x, 128 devices: a whole 4x4x4 slice. The times are simulated.
128 devices in a mesh: req: 16 (over y, x), seq: 4 (over z), hid: 2 (over core).
Axes of the slice: x: 4, y: 4, z: 4, core: 2. Of those that a mesh axis runs over, the one named last changes fastest.
Arguments:
- tokens: bfloat16 [65536, 2048], P(('req', 'seq')), may hold values from -6 to 6
- attention_gain: bfloat16 [2048], replicated, may hold values from 0.099609375 to 1.8984375
- project_weight: bfloat16 [2048, 2048], P(None, 'hid'), may hold values from -0.125 to 0.125
- conv_weight: bfloat16 [4, 2048], P(None, 'hid'), may hold values from -3 to 3
- decay_down: bfloat16 [2048, 16], replicated, may hold values from -0.125 to 0.125
- decay_up: bfloat16 [16, 512], P(None, 'hid'), may hold values from -1.5 to 1.5
- decay_bias: float32 [512], P('hid'), may hold values from -2 to 10
- output_gate: bfloat16 [2048, 1024], P(None, 'hid'), may hold values from -0.125 to 0.125
- head_gain: bfloat16 [512], replicated, may hold values from 0.099609375 to 1.8984375
- output_weight: bfloat16 [1024, 2048], P('hid'), may hold values from -0.1875 to 0.1875
- mixer_gain: bfloat16 [2048], replicated, may hold values from 0.099609375 to 1.8984375
- gate_weight: bfloat16 [2048, 2816], P('req', 'hid'), may hold values from -0.125 to 0.125
- up_weight: bfloat16 [2048, 2816], P('req', 'hid'), may hold values from -0.125 to 0.125
- down_weight: bfloat16 [2816, 2048], P('hid', 'req'), may hold values from -0.109375 to 0.109375
- prompt_pages: int32 [16, 16], P('req'), may hold values from 0 to 64, as said below
- prompt_start: int32 [16, 16], P('req'), may hold values from 0 to 63, as said below
Outputs:
- hidden_out: bfloat16 [65536, 2048], P(('req', 'seq', 'hid'))
- page_states: bfloat16 [1024, 2, 256, 512], P(('req', 'seq'), 'hid')
- conv_edges: bfloat16 [1024, 3, 2048], P(('req', 'seq'), None, 'hid')
Inputs may be any that keep to these rules, and one draw needn't show every extreme that they name: `prompt_pages`: row r lists the page counts of the prompts of group r; 0 marks an unused slot; in every draw some group holds one prompt of all its 64 pages. `prompt_start`: the slots of a row that are used cover pages in increasing order without intersection and end by page 64; pages between prompts belong to none; an unused slot starts at page 64 - 1, and every draw has one.
All inputs are finite; a program needn't handle non-finite values.
Results may differ from a plain program's by a relative error of at most 0.014.
Values may be sent and summed in bfloat16 or wider, within the bound.
A program may use at most 192 MiB of HBM per device.

v0:
```python
import jax
import jax.numpy as jnp
from jax import lax
from jax.sharding import PartitionSpec as P

HK = 256
HV = 512
KCONV = 4
PAGE = 64
CONVW = 1024
EPSILON = 1e-06
TOP_PRECISION = lax.Precision.HIGHEST


def shifted(value, axis, steps):
    count = lax.axis_size(axis)
    first, last = (max(0, -steps), min(count, count - steps))
    return lax.ppermute(value, axis, [(source, source + steps) for source in range(first, last)])


def prefix_2(array, axis, join, neutral):
    place = lax.axis_index(axis)
    gathered = jax.tree.map(
        lambda a, kind: lax.all_gather(a.astype(kind), axis), array, (jnp.bfloat16, jnp.bfloat16)
    )
    state = jax.tree.map(lambda a, e: jnp.zeros_like(a) + jnp.asarray(e, a.dtype), array, neutral)

    def one(lap, state):
        return join(
            state,
            jax.tree.map(
                lambda a, own: lax.dynamic_index_in_dim(a, lap, 0, False).astype(own.dtype),
                gathered,
                array,
            ),
        )

    return lax.fori_loop(0, place, one, state)


def rms_scaled(values, scale_gain):
    values = values.astype(jnp.float32)
    return (
        values
        * lax.rsqrt(jnp.mean(values * values, axis=-1, keepdims=True) + EPSILON)
        * scale_gain.astype(jnp.float32)
    )


def page_segments(page_counts, starts, total_pages):
    position = jnp.arange(total_pages, dtype=jnp.int32)
    inside = (position[None, :] >= starts[:, None]) & (
        position[None, :] < starts[:, None] + page_counts[:, None]
    )
    labels = jnp.arange(1, page_counts.shape[0] + 1, dtype=jnp.int32)
    segment = jnp.sum(jnp.where(inside, labels[:, None], 0), axis=0) - 1
    earlier = jnp.concatenate([jnp.full((1,), -1, jnp.int32), segment[:-1]])
    return ((segment == earlier) & (segment >= 0)).astype(jnp.float32)


def short_conv(by_page, before, carried, conv_taps):
    kept_rows = before.astype(jnp.float32) * carried[:, None, None]
    widened = jnp.concatenate([kept_rows, by_page.astype(jnp.float32)], axis=1)
    tap_count = conv_taps.shape[0]
    length = by_page.shape[1]
    result = jnp.zeros(by_page.shape, jnp.float32)
    for offset in range(tap_count):
        result = (
            result
            + conv_taps[offset].astype(jnp.float32)
            * widened[:, tap_count - 1 - offset : tap_count - 1 - offset + length]
        )
    return result


def split_features(mixed_rows, key_width):
    query_rows = jax.nn.silu(mixed_rows[..., :key_width])
    key_rows = jax.nn.silu(mixed_rows[..., key_width : 2 * key_width]) * key_width ** (-0.5)
    value_matrix = mixed_rows[..., 2 * key_width :]
    return (
        query_rows.transpose(0, 2, 1, 3),
        key_rows.transpose(0, 2, 1, 3),
        value_matrix.transpose(0, 2, 1, 3),
    )


def page_block(query_rows, key_rows, value_matrix, decay_sum, carried):
    length = query_rows.shape[2]
    page_count = query_rows.shape[0]
    raised_rows = query_rows * jnp.exp(decay_sum)
    lowered = key_rows * jnp.exp(-decay_sum)
    scores = jnp.einsum("phik,phjk->phij", raised_rows, lowered, precision=TOP_PRECISION)
    rows_index = jnp.arange(length)
    causal = rows_index[:, None] >= rows_index[None, :]
    scores = jnp.where(causal[None, None], scores, 0.0)
    layer_output = jnp.einsum("phij,phjv->phiv", scores, value_matrix, precision=TOP_PRECISION)
    closing_sum = decay_sum[:, :, -1, :]
    weighted_rows = key_rows * jnp.exp(closing_sum[:, :, None, :] - decay_sum)
    page_terms = jnp.einsum("phte,phtb->pheb", weighted_rows, value_matrix, precision=TOP_PRECISION)
    through = jnp.cumsum(closing_sum, axis=0)
    resets = jnp.cumsum(1.0 - carried)
    pages = jnp.arange(page_count)
    valid = (pages[:, None] >= pages[None, :]) & (resets[:, None] == resets[None, :])
    spread = through[:, None] - through[None, :]
    spread = jnp.where(valid[:, :, None, None], spread, 0.0)
    weights = jnp.where(valid[:, :, None, None], jnp.exp(spread), 0.0)
    memories = jnp.einsum("pqhe,qheb->pheb", weights, page_terms, precision=TOP_PRECISION)
    previous = jnp.concatenate([jnp.zeros_like(memories[:1]), memories[:-1]], axis=0)
    previous = previous * carried[:, None, None, None]
    layer_output = layer_output + jnp.einsum(
        "phik,phkv->phiv", raised_rows, previous, precision=TOP_PRECISION
    )
    return (memories[-1], layer_output, memories)


def on_device(
    tokens,
    attention_gain,
    project_weight,
    conv_weight,
    decay_down,
    decay_up,
    decay_bias,
    output_gate,
    head_gain,
    output_weight,
    mixer_gain,
    gate_weight,
    up_weight,
    down_weight,
    prompt_pages,
    prompt_start,
):
    token_count = tokens.shape[0]
    page_count = token_count // PAGE
    local_heads = project_weight.shape[1] // CONVW
    rim_rows = KCONV - 1
    seq_index = lax.axis_index("seq")
    group_pages = page_count * lax.axis_size("seq")
    page_flags = page_segments(prompt_pages[0], prompt_start[0], group_pages)
    carried = lax.dynamic_slice_in_dim(page_flags, seq_index * page_count, page_count)
    normed = rms_scaled(tokens, attention_gain).astype(jnp.bfloat16)
    projected = jnp.dot(normed, project_weight, preferred_element_type=jnp.float32).astype(
        jnp.bfloat16
    )
    by_page = projected.reshape(page_count, PAGE, local_heads * CONVW)
    incoming = shifted(by_page[-1, PAGE - rim_rows :], "seq", 1)
    before = jnp.concatenate([incoming[None], by_page[:-1, PAGE - rim_rows :]], axis=0)
    mixed_rows = short_conv(by_page, before, carried, conv_weight).reshape(
        page_count, PAGE, local_heads, CONVW
    )
    query_rows, key_rows, value_matrix = split_features(mixed_rows, HK)
    gate_rows = lax.all_gather(gate_weight, "req", axis=0, tiled=True)
    up_rows = lax.all_gather(up_weight, "req", axis=0, tiled=True)
    down_columns = lax.all_gather(down_weight, "req", axis=1, tiled=True)
    gate_rows, query_rows = lax.optimization_barrier((gate_rows, query_rows))
    lowrank = jnp.dot(normed, decay_down, preferred_element_type=jnp.float32).astype(jnp.bfloat16)
    decay_log = (
        jax.nn.log_sigmoid(
            jnp.dot(lowrank, decay_up, preferred_element_type=jnp.float32) + decay_bias
        )
        / 16.0
    )
    decay_log = decay_log.reshape(page_count, PAGE, local_heads, HK).transpose(0, 2, 1, 3)
    decay_sum = jnp.cumsum(decay_log, axis=2)
    local_memory, outputs, memories = page_block(
        query_rows, key_rows, value_matrix, decay_sum, carried
    )
    totals = decay_sum[:, :, -1, :]
    through = jnp.cumsum(totals, axis=0)
    alive_mask = jnp.cumprod(carried)
    block_decay = alive_mask[-1] * jnp.exp(through[-1])

    def compose(earlier, latter):
        return (earlier[0] * latter[0], latter[0][..., None] * earlier[1] + latter[1])

    prefix = prefix_2(
        (block_decay, local_memory),
        "seq",
        compose,
        (jnp.ones_like(block_decay), jnp.zeros_like(local_memory)),
    )
    incoming_state = prefix[1]
    before_sum = through - totals
    extent_factor = alive_mask[:, None, None, None] * jnp.exp(decay_sum + before_sum[:, :, None, :])
    outputs = outputs + jnp.einsum(
        "dlof,lfg->dlog", query_rows * extent_factor, incoming_state, precision=TOP_PRECISION
    )
    memories = (
        memories + (alive_mask[:, None, None] * jnp.exp(through))[..., None] * incoming_state[None]
    )
    up_rows, outputs = lax.optimization_barrier((up_rows, outputs))
    attended = outputs.transpose(0, 2, 1, 3).reshape(token_count, local_heads, HV)
    normed_heads = rms_scaled(attended, head_gain)
    opening = jax.nn.silu(jnp.dot(normed, output_gate, preferred_element_type=jnp.float32)).reshape(
        token_count, local_heads, HV
    )
    gated_rows = (
        (normed_heads * opening).astype(jnp.bfloat16).reshape(token_count, local_heads * HV)
    )
    down_columns, gated_rows = lax.optimization_barrier((down_columns, gated_rows))
    partial_value = jnp.dot(gated_rows, output_weight, preferred_element_type=jnp.float32)
    half_rows = token_count // lax.axis_size("hid")
    row_start = lax.axis_index("hid") * half_rows
    mixed_sum = lax.psum(partial_value.astype(jnp.bfloat16), "hid").astype(jnp.float32)
    residual = (tokens.astype(jnp.float32) + mixed_sum).astype(jnp.bfloat16)
    feed_in = rms_scaled(residual, mixer_gain).astype(jnp.bfloat16)
    own_residual = lax.dynamic_slice_in_dim(residual, row_start, half_rows, 0)

    def widen(weight_rows):
        return jnp.dot(feed_in, weight_rows, preferred_element_type=jnp.float32)

    gate_part = widen(gate_rows)
    up_part = widen(up_rows)
    hidden = (jax.nn.silu(gate_part) * up_part).astype(jnp.bfloat16)
    partials = jnp.dot(hidden, down_columns, preferred_element_type=jnp.float32)
    feed_sum = lax.psum_scatter(
        partials.astype(jnp.bfloat16), "hid", scatter_dimension=0, tiled=True
    ).astype(jnp.float32)
    result = (own_residual.astype(jnp.float32) + feed_sum).astype(jnp.bfloat16)
    return (result, memories.astype(jnp.bfloat16), by_page[:, PAGE - rim_rows :])


def solution(mesh):
    return jax.shard_map(
        on_device,
        mesh=mesh,
        in_specs=(
            P(("req", "seq"), None),
            P(),
            P(None, "hid"),
            P(None, "hid"),
            P(),
            P(None, "hid"),
            P("hid"),
            P(None, "hid"),
            P(),
            P("hid", None),
            P(),
            P("req", "hid"),
            P("req", "hid"),
            P("hid", "req"),
            P("req", None),
            P("req", None),
        ),
        out_specs=(
            P(("req", "seq", "hid"), None),
            P(("req", "seq"), "hid", None, None),
            P(("req", "seq"), None, "hid"),
        ),
        check_vma=False,
    )
```

profile of v0, /device:TPU:1, one launch (start us, length us, event | category | flops | bytes accessed | tf_op | source)
XLA Modules:
  0.0 392.0 jit_solution(12662995687886767372)
XLA Ops:
  7.2 3.2 fusion.3
  10.5 0.3 copy-done.7
  10.8 7.3 %convolution_convert_fusion.2 = bf16[1024,1024]{1,0:T(8,128)(2,1)S(1)} fusion(bf16[2048,1024]{1,0:T(8,128)(2,1)} %param.20, bf16[1024,2048]{1,0:T(8,128)(2,1)S(1)} %copy-done.7, f32[2048]{0:T(1024)S(1)} %convert_element_type.149, f32[1024]{0:T(1024)S(1)} %add_rsqrt_fusion.2), kind=kOutput, calls=%fused_computation.53 | convolution fusion | flops 4304404480 | bytes 10498048 | tf_op jit(solution)/shard_map/dot_general | solution.py:143
  18.1 1.3 copy-done.10
  19.4 4.4 %collective-permute-start = (bf16[3,1024]{1,0:T(4,128)(2,1)S(1)}, bf16[3,1024]{1,0:T(4,128)(2,1)S(1)}, u32[]{:S(2)}, u32[]{:S(2)}) collective-permute-start(bf16[3,1024]{1,0:T(4,128)(2,1)S(1)} %slice_bitcast_fusion.5), channel_id=1, source_target_pairs={{0,2},{2,4},{4,6},{1,3},{3,5},{5,7},{8,10},{10,12},{12,14},{9,11},... | collective-permute-start | bytes 18440 | tf_op jit(solution)/shard_map/ppermute | solution.py:18
  24.0 5.2 %fusion.37 = f32[1024,256]{1,0:T(8,128)} fusion(bf16[16,256]{1,0:T(8,128)(2,1)S(1)} %copy-done.18, bf16[2048,16]{0,1:T(8,128)(2,1)S(1)} %copy-done.17, f32[256]{0:T(256)S(1)} %copy-done.19, bf16[1024,2048]{1,0:T(8,128)(2,1)} %param.18, f32[2048]{0:T(1024)S(1)} %convert_element_type.149, f32[1024]{0:T(1024)S(1)} %add_rsqrt_fusion.2), kind=kOutput, calls=%fused_computation.60 | convolution fusion | flops 86523904 | bytes 5329920 | tf_op jit(solution)/shard_map/dot_general | solution.py:160
  29.2 1.8 fusion.49
  31.4 0.1 reduce.2
  31.6 1.0 slice.80
  32.6 4.1 %convert_element_type.152 = f32[16,64,1024]{2,1,0:T(8,128)} convert(bf16[16,64,1024]{2,1,0:T(8,128)(2,1)} %bitcast.123) | non-fusion elementwise | flops 1048576 | bytes 6291456 | tf_op jit(solution)/shard_map/convert_element_type | solution.py:63
  36.9 7.6 %fusion.15 = f32[16,64,1,1024]{3,1,0,2:T(8,128)S(1)} fusion(f32[16,64,1024]{2,1,0:T(8,128)} %convert_element_type.152, f32[16,3,1024]{2,1,0:T(4,128)S(1)} %convert_multiply_fusion.4, f32[1024]{0:T(1024)S(1)} %bitcast.130, f32[1024]{0:T(1024)S(1)} %bitcast.131, f32[1024]{0:T(1024)S(1)} %bitcast.129, f32[1024]{0:T(1024)S(1)} %bitcast.128), kind=kLoop, calls=%fused_computation.29 | loop fusion | flops 10485760 | bytes 8601600 | tf_op jit(solution)/shard_map/reshape | solution.py:149
  44.6 7.4 %fusion.30 = f32[16,256,512]{2,1,0:T(8,128)S(1)} fusion(f32[16,64,1,1024]{3,1,0,2:T(8,128)S(1)} %fusion.15, f32[16,1,64,256]{3,0,1,2:T(8,128)S(1)} %fusion.49, f32[16,256]{1,0:T(8,128)S(1)} %get-tuple-element.97), kind=kOutput, calls=%fused_computation.51 | convolution fusion | flops 1612447744 | bytes 12599296 | tf_op jit(solution)/shard_map/phte,phtb->pheb/dot_general | solution.py:99
  52.0 13.6 %fusion.20 = f32[16,1,256,512]{3,0,2,1:T(8,128)S(1)} fusion(f32[16,256,512]{2,1,0:T(8,128)S(1)} %fusion.30, f32[16,256]{0,1:T(8,128)S(1)} %bitcast.125, pred[16,16]{1,0:T(8,128)(4,1)S(1)} %fusion.72), kind=kOutput, calls=%fused_computation.38 | convolution fusion | flops 402849792 | bytes 16793856 | tf_op jit(solution)/shard_map/pqhe,qheb->pheb/dot_general | solution.py:107
  65.6 3.2 copy-done.2
  68.8 0.6 slice.145
  69.4 0.7 copy.72
  70.2 0.7 all-gather.9.cloned.1.call-update
  70.9 0.7 all-gather.7.cloned.1.call-update
  71.7 0.5 all-gather.5.cloned.1.call-update
  72.4 0.5 slice.90
  73.0 0.6 fusion.74
  73.7 6.9 %all_gather.20 = bf16[4,1,256]{2,1,0:T(2,128)(2,1)S(1)} all-gather(bf16[1,1,256]{2,1,0:T(2,128)(2,1)S(1)} %fusion.74), channel_id=1, replica_groups=mesh['req'=16,'seq'=4,'hid'=2] {'seq'}, dimensions={0}, use_global_device_ids=true | all-gather | bytes 2560 | tf_op jit(solution)/shard_map/all_gather | solution.py:24
  80.6 2.5 multiply_bitcast_fusion.1
  83.1 8.6 %multiply_bitcast_fusion = f32[16,256,512]{2,0,1:T(8,128)} fusion(f32[15,1,256,512]{3,0,2,1:T(8,128)} %bitcast.119, f32[16]{0:T(128)S(1)} %get-tuple-element.95), kind=kLoop, calls=%fused_computation.19 | loop fusion | flops 2097152 | bytes 16252992 | tf_op jit(solution)/shard_map/reshape.33
  91.7 4.1 %all-gather.11.cloned.1.call-done = bf16[4,1,256,512]{3,2,1,0:T(8,128)(2,1)} async-done(((bf16[1,1,256,512]{3,2,1,0:T(8,128)(2,1)}), bf16[4,1,256,512]{3,2,1,0:T(8,128)(2,1)}) %all-gather.11.cloned.1.call-update) | async-done | bytes 1048592 | tf_op jit(solution)/shard_map/all_gather | solution.py:24
  95.8 0.2 while.12
  96.0 62.0 %all-gather.9.cloned.1.call-done = bf16[2048,1408]{1,0:T(8,128)(2,1)} async-done(((bf16[128,1408]{1,0:T(8,128)(2,1)}), bf16[2048,1408]{1,0:T(8,128)(2,1)}) %all-gather.9.cloned.1.call-update) | async-done | bytes 5767184 | tf_op jit(solution)/shard_map/all_gather | solution.py:153
  158.0 4.7 %convolution_select_fusion = f32[16,64,64]{2,1,0:T(8,128)S(1)} fusion(f32[16,1,64,256]{3,2,0,1:T(8,128)} %multiply_bitcast_fusion.1, f32[16,1,64,256]{3,0,1,2:T(8,128)} %copy-done.5, pred[64,64]{1,0:T(8,128)(4,1)S(1)} %iota_compare_fusion, f32[16,64,1,1024]{3,1,0,2:T(8,128)} %copy-done.4), kind=kOutput, calls=%fused_computation.56 | convolution fusion | flops 203489280 | bytes 4460544 | tf_op jit(solution)/shard_map/phik,phjk->phij/dot_general | solution.py:92
  162.7 3.4 fusion.31
  166.2 10.6 %fusion.7 = f32[16,64,512]{2,1,0:T(8,128)S(1)} fusion(f32[16,256,512]{2,0,1:T(8,128)S(1)} %copy-done.3, f32[16,1,64,256]{3,2,0,1:T(8,128)S(1)} %copy-done.8, f32[16,1,64,256]{3,0,1,2:T(8,128)S(1)} %copy-done.6), kind=kOutput, calls=%fused_computation.14 | convolution fusion | flops 1610874880 | bytes 12582912 | tf_op jit(solution)/shard_map/phik,phkv->phiv/dot_general | solution.py:110
  176.7 3.9 bitcast_add_fusion
  180.6 38.0 %all-gather.7.cloned.1.call-done = bf16[2048,1408]{1,0:T(8,128)(2,1)} async-done(((bf16[128,1408]{1,0:T(8,128)(2,1)}), bf16[2048,1408]{1,0:T(8,128)(2,1)}) %all-gather.7.cloned.1.call-update) | async-done | bytes 5767184 | tf_op jit(solution)/shard_map/all_gather | solution.py:154
  218.6 1.8 multiply_reduce_fusion
  220.5 7.1 %fusion.25 = bf16[1024,512]{1,0:T(8,128)(2,1)} fusion(f32[16,1,64,512]{3,2,0,1:T(8,128)} %bitcast_add_fusion, f32[512]{0:T(512)S(1)} %convert_element_type.163, f32[1024]{0:T(1024)S(1)} %rsqrt.29, bf16[2048,512]{1,0:T(8,128)(2,1)} %param.25, bf16[1024,2048]{1,0:T(8,128)(2,1)} %param.18, f32[2048]{0:T(1024)S(1)} %convert_element_type.149, ...), kind=kOutput, calls=%fused_computation.45 | convolution fusion | flops 2160066560 | bytes 9455616 | tf_op jit(solution)/shard_map/dot_general | solution.py:195
  227.6 56.9 %all-gather.5.cloned.1.call-done = bf16[1408,2048]{1,0:T(8,128)(2,1)} async-done(((bf16[1408,128]{1,0:T(8,128)(2,1)}), bf16[1408,2048]{1,0:T(8,128)(2,1)}) %all-gather.5.cloned.1.call-update) | async-done | bytes 5767184 | tf_op jit(solution)/shard_map/all_gather | solution.py:155
  284.5 5.6 %convolution_convert_fusion.1 = bf16[1024,2048]{1,0:T(8,128)(2,1)} fusion(bf16[1024,512]{1,0:T(8,128)(2,1)} %fusion.25, bf16[512,2048]{1,0:T(8,128)(2,1)S(1)} %copy-done), kind=kOutput, calls=%fused_computation.37 | convolution fusion | flops 2149580800 | bytes 7340032 | tf_op jit(solution)/shard_map/dot_general | solution.py:202
  290.2 0.6 copy-done.13
  290.8 34.2 %all-reduce.3.cloned.1.call-done = bf16[1024,2048]{1,0:T(8,128)(2,1)} async-done(((bf16[1024,2048]{1,0:T(8,128)(2,1)}), bf16[1024,2048]{1,0:T(8,128)(2,1)}) %all-reduce.3.cloned.1.call-update) | async-done | bytes 4194320 | tf_op jit(solution)/shard_map/psum | solution.py:205
  325.0 5.5 %fusion = (f32[1024]{0:T(1024)S(1)}, bf16[1024,2048]{1,0:T(8,128)(2,1)S(1)}) fusion(bf16[1024,2048]{1,0:T(8,128)(2,1)} %all-reduce.3.cloned.1.call-done, bf16[1024,2048]{1,0:T(8,128)(2,1)} %param.18), kind=kLoop, calls=%fused_computation.7 | loop fusion | flops 14679040 | bytes 12587008 | tf_op jit(solution)/shard_map/reduce_sum | solution.py:45
  330.5 2.0 copy-done.9
  332.5 10.7 %fusion.34 = f32[1024,1408]{1,0:T(8,128)} fusion(bf16[2048,1408]{1,0:T(8,128)(2,1)} %all-gather.9.cloned.1.call-done, bf16[1024,2048]{1,0:T(8,128)(2,1)S(1)} %get-tuple-element.93, f32[2048]{0:T(1024)S(1)} %convert_element_type.170, f32[1024]{0:T(1024)S(1)} %add_rsqrt_fusion.1), kind=kOutput, calls=%fused_computation.57 | convolution fusion | flops 5913968640 | bytes 15740928 | tf_op jit(solution)/shard_map/dot_general | solution.py:211
  343.2 20.9 %convolution_convert_fusion = bf16[1024,2048]{1,0:T(8,128)(2,1)} fusion(bf16[1408,2048]{1,0:T(8,128)(2,1)} %all-gather.5.cloned.1.call-done, f32[1024,1408]{1,0:T(8,128)} %fusion.34, bf16[2048,1408]{1,0:T(8,128)(2,1)} %all-gather.7.cloned.1.call-done, bf16[1024,2048]{1,0:T(8,128)(2,1)} %copy-done.9, f32[2048]{0:T(1024)S(1)} %convert_element_type.170, ...), kind=kOutput, calls=%fused_computation.36 | convolution fusion | flops 11830296576 | bytes 25702400 | tf_op jit(solution)/shard_map/dot_general | solution.py:216
  364.1 1.0 slice.93
  365.3 0.7 copy.76
  366.0 4.0 %add_convert_fusion = bf16[16,1,256,512]{3,0,2,1:T(8,128)(2,1)S(1)} fusion(f32[16,1,256,512]{3,0,2,1:T(8,128)} %copy-done.2, f32[256,512]{1,0:T(8,128)S(1)} %bitcast.120, f32[16,256]{0,1:T(8,128)S(1)} %copy.74), kind=kLoop, calls=%fused_computation.18 | loop fusion | flops 6291456 | bytes 13123584 | tf_op jit(solution)/shard_map/convert_element_type | solution.py:221
  370.0 4.5 %copy.75 = bf16[16,1,256,512]{3,2,1,0:T(8,128)(2,1)} copy(bf16[16,1,256,512]{3,0,2,1:T(8,128)(2,1)S(1)} %add_convert_fusion) | data formatting | bytes 8388608
  374.5 5.8 %reduce-scatter.2.cloned.1.call-done = bf16[512,2048]{1,0:T(8,128)(2,1)} async-done(((bf16[1024,2048]{1,0:T(8,128)(2,1)}), bf16[512,2048]{1,0:T(8,128)(2,1)}) %reduce-scatter.2.cloned.1.call-update) | async-done | bytes 2097168 | tf_op jit(solution)/shard_map/reduce_scatter | solution.py:217
  380.3 4.4 %add_convert_fusion.1 = bf16[512,2048]{1,0:T(8,128)(2,1)} fusion(bf16[512,2048]{1,0:T(8,128)(2,1)} %reduce-scatter.2.cloned.1.call-done, bf16[1024,2048]{1,0:T(8,128)(2,1)} %copy-done.9, s32[]{:T(128)S(6)} %select_n.46), kind=kLoop, calls=%fused_computation.35 | loop fusion | flops 4194304 | bytes 6291460 | tf_op jit(solution)/shard_map/convert_element_type | solution.py:220
  (74 shorter events, 1.7 us)
Async XLA Ops:
  7.2 277.4 %copy-start = (bf16[512,2048]{1,0:T(8,128)(2,1)S(1)}, bf16[512,2048]{1,0:T(8,128)(2,1)}, u32[]{:S(2)}) copy-start(bf16[512,2048]{1,0:T(8,128)(2,1)} %param.27) | copy-start | bytes 6291460
  7.2 3.3 copy-start.12
  7.2 88.6 %all-gather.11.cloned.1.call-start = ((), (), s32[]{:S(2)}) async-start(), calls=%async_computation.4 | async-start | bytes 1310720 | tf_op jit(solution)/shard_map/all_gather | solution.py:24
  7.2 3.6 copy-start.7
  10.8 13.0 %copy-start.14 = (s32[1,16]{1,0:T(1,128)S(1)}, s32[1,16]{1,0:T(1,128)}, u32[]{:S(2)}) copy-start(s32[1,16]{1,0:T(1,128)} %param.33) | copy-start | bytes 196
  10.8 13.0 %copy-start.16 = (s32[1,16]{1,0:T(1,128)S(1)}, s32[1,16]{1,0:T(1,128)}, u32[]{:S(2)}) copy-start(s32[1,16]{1,0:T(1,128)} %param.32) | copy-start | bytes 196
  10.8 13.2 %copy-start.11 = (bf16[4,1024]{1,0:T(4,128)(2,1)S(1)}, bf16[4,1024]{1,0:T(4,128)(2,1)}, u32[]{:S(2)}) copy-start(bf16[4,1024]{1,0:T(4,128)(2,1)} %param.21) | copy-start | bytes 24580
  10.8 13.2 %copy-start.17 = (bf16[2048,16]{0,1:T(8,128)(2,1)S(1)}, bf16[2048,16]{0,1:T(8,128)(2,1)}, u32[]{:S(2)}) copy-start(bf16[2048,16]{0,1:T(8,128)(2,1)} %param.22) | copy-start | bytes 196612
  10.8 13.2 %copy-start.18 = (bf16[16,256]{1,0:T(8,128)(2,1)S(1)}, bf16[16,256]{1,0:T(8,128)(2,1)}, u32[]{:S(2)}) copy-start(bf16[16,256]{1,0:T(8,128)(2,1)} %param.23) | copy-start | bytes 24580
  10.8 13.2 %copy-start.19 = (f32[256]{0:T(256)S(1)}, f32[256]{0:T(256)}, u32[]{:S(2)}) copy-start(f32[256]{0:T(256)} %param.24) | copy-start | bytes 3076
  18.1 1.3 copy-start.10
  19.4 17.3 %collective-permute-start = (bf16[3,1024]{1,0:T(4,128)(2,1)S(1)}, bf16[3,1024]{1,0:T(4,128)(2,1)S(1)}, u32[]{:S(2)}, u32[]{:S(2)}) collective-permute-start(bf16[3,1024]{1,0:T(4,128)(2,1)S(1)} %slice_bitcast_fusion.5), channel_id=1, source_target_pairs={{0,2},{2,4},{4,6},{1,3},{3,5},{5,7},{8,10},{10,12},{12,14},{9,11},... | collective-permute-start | bytes 18440 | tf_op jit(solution)/shard_map/ppermute | solution.py:18
  31.0 13.5 %copy-start.5 = (f32[16,1,64,256]{3,0,1,2:T(8,128)}, f32[16,1,64,256]{3,0,1,2:T(8,128)S(1)}, u32[]{:S(2)}) copy-start(f32[16,1,64,256]{3,0,1,2:T(8,128)S(1)} %fusion.49) | copy-start | bytes 3145732
  44.6 7.4 %copy-start.4 = (f32[16,64,1,1024]{3,1,0,2:T(8,128)}, f32[16,64,1,1024]{3,1,0,2:T(8,128)S(1)}, u32[]{:S(2)}) copy-start(f32[16,64,1,1024]{3,1,0,2:T(8,128)S(1)} %fusion.15) | copy-start | bytes 12582916
  52.0 21.1 %copy-start.15 = (bf16[512]{0:T(512)(128)(2,1)S(1)}, bf16[512]{0:T(512)(128)(2,1)}, u32[]{:S(2)}) copy-start(bf16[512]{0:T(512)(128)(2,1)} %param.26) | copy-start | bytes 3076
  65.6 3.2 copy-start.2
  70.1 87.9 %all-gather.9.cloned.1.call-start = ((), (), s32[]{:S(2)}) async-start(), calls=%async_computation.3 | async-start | bytes 6127616 | tf_op jit(solution)/shard_map/all_gather | solution.py:153
  70.9 147.7 %all-gather.7.cloned.1.call-start = ((), (), s32[]{:S(2)}) async-start(), calls=%async_computation.2 | async-start | bytes 6127616 | tf_op jit(solution)/shard_map/all_gather | solution.py:154
  71.6 212.9 %all-gather.5.cloned.1.call-start = ((), (), s32[]{:S(2)}) async-start(), calls=%async_computation.1 | async-start | bytes 6127616 | tf_op jit(solution)/shard_map/all_gather | solution.py:155
  72.2 252.8 %all-reduce.3.cloned.1.call-start = ((), (), s32[]{:S(2)}) async-start(), calls=%async_computation.5 | async-start | bytes 8388608 | tf_op jit(solution)/shard_map/psum | solution.py:205
  158.0 8.2 %copy-start.3 = (f32[16,256,512]{2,0,1:T(8,128)S(1)}, f32[16,256,512]{2,0,1:T(8,128)}, u32[]{:S(2)}) copy-start(f32[16,256,512]{2,0,1:T(8,128)} %multiply_bitcast_fusion) | copy-start | bytes 25165828
  158.0 8.2 %copy-start.6 = (f32[16,1,64,256]{3,0,1,2:T(8,128)S(1)}, f32[16,1,64,256]{3,0,1,2:T(8,128)}, u32[]{:S(2)}) copy-start(f32[16,1,64,256]{3,0,1,2:T(8,128)} %copy-done.5) | copy-start | bytes 3145732
  158.0 8.2 %copy-start.8 = (f32[16,1,64,256]{3,2,0,1:T(8,128)S(1)}, f32[16,1,64,256]{3,2,0,1:T(8,128)}, u32[]{:S(2)}) copy-start(f32[16,1,64,256]{3,2,0,1:T(8,128)} %multiply_bitcast_fusion.1) | copy-start | bytes 3145732
  290.1 0.7 copy-start.13
  290.2 90.2 %reduce-scatter.2.cloned.1.call-start = ((), (), s32[]{:S(2)}) async-start(), calls=%async_computation.6 | async-start | bytes 6291456 | tf_op jit(solution)/shard_map/reduce_scatter | solution.py:217
  330.5 2.0 copy-start.9
  370.0 14.8 %copy-start.1 = (bf16[512,2048]{1,0:T(8,128)(2,1)S(1)}, bf16[512,2048]{1,0:T(8,128)(2,1)}, u32[]{:S(2)}) copy-start(bf16[512,2048]{1,0:T(8,128)(2,1)} %param.27) | copy-start | bytes 6291460
Sparse Core Ops, SparseCore 0:
  70.2 25.4 all-gather.10
  97.9 60.0 all-gather.8
  160.1 58.4 all-gather.6
  220.6 63.9 all-gather.4
  290.3 34.7 all-reduce.2
  364.2 16.0 reduce-scatter.1
where the time goes:
time: 398 us; the launch traced here: 392 us
  waiting for transfers between devices  203 us (51%)
  matrix products  100 us (25%)
  other arithmetic  45.1 us (11%)
  local copies, waits for them, and re-layouts  17 us (4%)
  between operations  15 us (4%)
  blocking collectives  6.9 us (2%)
  starting transfers between devices  4.61 us (1%)
    all_gather x1, waiting for transfers between devices, on_device(): gate_rows = lax.all_gather(gate_weight, 'req', axis=0, tiled=True)  62 us
    all_gather x1, waiting for transfers between devices, on_device(): down_columns = lax.all_gather(down_weight, 'req', axis=1, tiled=True)  56.9 us
    all_gather x1, waiting for transfers between devices, on_device(): up_rows = lax.all_gather(up_weight, 'req', axis=0, tiled=True)  38 us
    psum x1, waiting for transfers between devices, on_device(): lax.psum(partial_value.astype(jnp.bfloat16), 'hid').astype(jnp.float32)  34.2 us
    dot_general x1, matrix products, on_device(): partials = jnp.dot(hidden, down_columns, preferred_element_type=jnp.float32)  20.9 us
    dot_general x1, matrix products, page_block(): jnp.einsum('pqhe,qheb->pheb', weights, page_terms, precision=TOP_PRECISION)  13.6 us
    unnamed x43, local copies, waits for them, and re-layouts  12.8 us
    dot_general x1, matrix products, widen(): return jnp.dot(feed_in, weight_rows, preferred_element_type=jnp.float32)  10.7 us
  transfers between devices with their start and end apart: 7, of which 6 were waited for; matrix products, arithmetic and copies ran while one was open for 17% of the time, Pallas kernels for 0%

commit v1 on v0

--- a/solution.py
+++ b/solution.py
@@ -151,7 +151,15 @@
     )
     query_rows, key_rows, value_matrix = split_features(mixed_rows, HK)
     gate_rows = lax.all_gather(gate_weight, "req", axis=0, tiled=True)
-    up_rows = lax.all_gather(up_weight, "req", axis=0, tiled=True)
+    up_rows = jnp.concatenate(
+        lax.all_to_all(
+            jnp.stack(lax.axis_size("req") * [up_weight]),
+            axis_name="req",
+            split_axis=0,
+            concat_axis=0,
+        ),
+        0,
+    )
     down_columns = lax.all_gather(down_weight, "req", axis=1, tiled=True)
     gate_rows, query_rows = lax.optimization_barrier((gate_rows, query_rows))
     lowrank = jnp.dot(normed, decay_down, preferred_element_type=jnp.float32).astype(jnp.bfloat16)

time: 398 us -> 381 us (0.957)
  waiting for transfers between devices: 203 us -> 175 us
  starting transfers between devices: 4.61 us -> 11.5 us
    all_gather x1 -> x0, waiting for transfers between devices: 38 us -> none  [on_device(): up_rows = lax.all_gather(up_weight, 'req', axis=0, tiled=True)]
    all_gather x1, waiting for transfers between devices: 62 us -> 99.3 us  [on_device(): gate_rows = lax.all_gather(gate_weight, 'req', axis=0, tiled=True)]
    all_gather x1, waiting for transfers between devices: 56.9 us -> 34.3 us  [on_device(): down_columns = lax.all_gather(down_weight, 'req', axis=1, tiled=True)]
    all_to_all x0 -> x1, starting transfers between devices: none -> 6.93 us  [on_device(): lax.all_to_all(jnp.stack(lax.axis_size('req') * [up_weight]), axis_name='...]
    all_gather x1, waiting for transfers between devices: 4.1 us -> 0.01 us  [prefix_2(): lax.all_gather(a.astype(kind), axis)]
    unnamed x43 -> x45, local copies, waits for them, and re-layouts: 12.8 us -> 12.8 us
  transfers between devices with their start and end apart: 7 -> 7, of which waited for: 6 -> 4; matrix products, arithmetic and copies ran while one was open for 17% -> 19% of each run, Pallas kernels for 0% -> 0%
where the time goes in v1:
time: 381 us; the launch traced here: 375 us
  waiting for transfers between devices  175 us (46%)
  matrix products  101 us (27%)
  other arithmetic  44.9 us (12%)
  local copies, waits for them, and re-layouts  20.1 us (5%)
  between operations  14.7 us (4%)
  starting transfers between devices  11.5 us (3%)
  blocking collectives  7.68 us (2%)
    all_gather x1, waiting for transfers between devices, on_device(): gate_rows = lax.all_gather(gate_weight, 'req', axis=0, tiled=True)  99.3 us
    all_gather x1, waiting for transfers between devices, on_device(): down_columns = lax.all_gather(down_weight, 'req', axis=1, tiled=True)  34.3 us
    psum x1, waiting for transfers between devices, on_device(): lax.psum(partial_value.astype(jnp.bfloat16), 'hid').astype(jnp.float32)  34.2 us
    dot_general x1, matrix products, on_device(): partials = jnp.dot(hidden, down_columns, preferred_element_type=jnp.float32)  20.9 us
    dot_general x1, matrix products, page_block(): jnp.einsum('pqhe,qheb->pheb', weights, page_terms, precision=TOP_PRECISION)  13.6 us
    unnamed x45, local copies, waits for them, and re-layouts  12.8 us
    dot_general x1, matrix products, widen(): return jnp.dot(feed_in, weight_rows, preferred_element_type=jnp.float32)  10.8 us
    dot_general x1, matrix products, page_block(): jnp.einsum('phik,phkv->phiv', raised_rows, previous, precision=TOP_PRECIS...  10.6 us
  transfers between devices with their start and end apart: 7, of which 4 were waited for; matrix products, arithmetic and copies ran while one was open for 19% of the time, Pallas kernels for 0%

profile of v1, /device:TPU:1, one launch (start us, length us, event | category | flops | bytes accessed | tf_op | source)
XLA Modules:
  0.0 374.7 jit_solution(18434760056850101774)
XLA Ops:
  7.2 3.2 fusion.3
  10.5 0.3 copy-done.7
  10.8 7.3 %convolution_convert_fusion.2 = bf16[1024,1024]{1,0:T(8,128)(2,1)S(1)} fusion(bf16[2048,1024]{1,0:T(8,128)(2,1)} %param.20, bf16[1024,2048]{1,0:T(8,128)(2,1)S(1)} %copy-done.7, f32[2048]{0:T(1024)S(1)} %convert_element_type.149, f32[1024]{0:T(1024)S(1)} %add_rsqrt_fusion.2), kind=kOutput, calls=%fused_computation.53 | convolution fusion | flops 4304404480 | bytes 10498048 | tf_op jit(solution)/shard_map/dot_general | solution.py:143
  18.1 1.3 copy-done.10
  19.4 4.4 %collective-permute-start = (bf16[3,1024]{1,0:T(4,128)(2,1)S(1)}, bf16[3,1024]{1,0:T(4,128)(2,1)S(1)}, u32[]{:S(2)}, u32[]{:S(2)}) collective-permute-start(bf16[3,1024]{1,0:T(4,128)(2,1)S(1)} %slice_bitcast_fusion.5), channel_id=1, source_target_pairs={{0,2},{2,4},{4,6},{1,3},{3,5},{5,7},{8,10},{10,12},{12,14},{9,11},... | collective-permute-start | bytes 18440 | tf_op jit(solution)/shard_map/ppermute | solution.py:18
  24.0 5.2 %fusion.37 = f32[1024,256]{1,0:T(8,128)} fusion(bf16[16,256]{1,0:T(8,128)(2,1)S(1)} %copy-done.19, bf16[2048,16]{0,1:T(8,128)(2,1)S(1)} %copy-done.18, f32[256]{0:T(256)S(1)} %copy-done.20, bf16[1024,2048]{1,0:T(8,128)(2,1)} %param.18, f32[2048]{0:T(1024)S(1)} %convert_element_type.149, f32[1024]{0:T(1024)S(1)} %add_rsqrt_fusion.2), kind=kOutput, calls=%fused_computation.60 | convolution fusion | flops 86523904 | bytes 5329920 | tf_op jit(solution)/shard_map/dot_general | solution.py:168
  29.2 1.8 fusion.49
  31.4 0.1 reduce.2
  31.6 1.0 slice.80
  32.6 4.1 %convert_element_type.152 = f32[16,64,1024]{2,1,0:T(8,128)} convert(bf16[16,64,1024]{2,1,0:T(8,128)(2,1)} %bitcast.124) | non-fusion elementwise | flops 1048576 | bytes 6291456 | tf_op jit(solution)/shard_map/convert_element_type | solution.py:63
  36.9 7.5 %fusion.15 = f32[16,64,1,1024]{3,1,0,2:T(8,128)S(1)} fusion(f32[16,64,1024]{2,1,0:T(8,128)} %convert_element_type.152, f32[16,3,1024]{2,1,0:T(4,128)S(1)} %convert_multiply_fusion.4, f32[1024]{0:T(1024)S(1)} %bitcast.131, f32[1024]{0:T(1024)S(1)} %bitcast.132, f32[1024]{0:T(1024)S(1)} %bitcast.130, f32[1024]{0:T(1024)S(1)} %bitcast.129), kind=kLoop, calls=%fused_computation.29 | loop fusion | flops 10485760 | bytes 8601600 | tf_op jit(solution)/shard_map/reshape | solution.py:149
  44.5 7.4 %fusion.30 = f32[16,256,512]{2,1,0:T(8,128)S(1)} fusion(f32[16,64,1,1024]{3,1,0,2:T(8,128)S(1)} %fusion.15, f32[16,1,64,256]{3,0,1,2:T(8,128)S(1)} %fusion.49, f32[16,256]{1,0:T(8,128)S(1)} %get-tuple-element.97), kind=kOutput, calls=%fused_computation.51 | convolution fusion | flops 1612447744 | bytes 12599296 | tf_op jit(solution)/shard_map/phte,phtb->pheb/dot_general | solution.py:99
  51.9 13.6 %fusion.20 = f32[16,1,256,512]{3,0,2,1:T(8,128)S(1)} fusion(f32[16,256,512]{2,1,0:T(8,128)S(1)} %fusion.30, f32[16,256]{0,1:T(8,128)S(1)} %bitcast.126, pred[16,16]{1,0:T(8,128)(4,1)S(1)} %fusion.72), kind=kOutput, calls=%fused_computation.38 | convolution fusion | flops 402849792 | bytes 16793856 | tf_op jit(solution)/shard_map/pqhe,qheb->pheb/dot_general | solution.py:107
  65.5 3.2 copy-done.2
  68.8 0.6 slice.145
  69.3 0.8 copy.72
  70.1 0.7 all-gather.6.cloned.1.call-update
  70.9 0.7 all-gather.4.cloned.1.call-update
  71.6 3.0 stack.2
  74.6 6.9 %all-to-all-start = ((bf16[16,128,1408]{2,1,0:T(8,128)(2,1)}), bf16[16,128,1408]{2,1,0:T(8,128)(2,1)}, u32[]{:S(2)}, u32[]{:S(2)}) async-start(bf16[16,128,1408]{2,1,0:T(8,128)(2,1)} %stack.2), calls=%async_computation | async-start | bytes 11534336 | tf_op jit(solution)/shard_map/all_to_all | solution.py:155
  81.8 0.5 slice.90
  82.3 0.1 reduce.3
  82.4 0.6 fusion.74
  83.0 7.7 %all_gather.16 = bf16[4,1,256]{2,1,0:T(2,128)(2,1)S(1)} all-gather(bf16[1,1,256]{2,1,0:T(2,128)(2,1)S(1)} %fusion.74), channel_id=1, replica_groups=mesh['req'=16,'seq'=4,'hid'=2] {'seq'}, dimensions={0}, use_global_device_ids=true | all-gather | bytes 2560 | tf_op jit(solution)/shard_map/all_gather | solution.py:24
  90.7 2.5 multiply_bitcast_fusion.1
  93.2 8.5 %multiply_bitcast_fusion = f32[16,256,512]{2,0,1:T(8,128)} fusion(f32[15,1,256,512]{3,0,2,1:T(8,128)} %bitcast.120, f32[16]{0:T(128)S(1)} %get-tuple-element.95), kind=kLoop, calls=%fused_computation.19 | loop fusion | flops 2097152 | bytes 16252992 | tf_op jit(solution)/shard_map/reshape.35
  101.8 0.2 while.12
  102.0 99.3 %all-gather.6.cloned.1.call-done = bf16[2048,1408]{1,0:T(8,128)(2,1)} async-done(((bf16[128,1408]{1,0:T(8,128)(2,1)}), bf16[2048,1408]{1,0:T(8,128)(2,1)}) %all-gather.6.cloned.1.call-update) | async-done | bytes 5767184 | tf_op jit(solution)/shard_map/all_gather | solution.py:153
  201.3 4.7 %convolution_select_fusion = f32[16,64,64]{2,1,0:T(8,128)S(1)} fusion(f32[16,1,64,256]{3,2,0,1:T(8,128)} %multiply_bitcast_fusion.1, f32[16,1,64,256]{3,0,1,2:T(8,128)} %copy-done.5, pred[64,64]{1,0:T(8,128)(4,1)S(1)} %iota_compare_fusion, f32[16,64,1,1024]{3,1,0,2:T(8,128)} %copy-done.4), kind=kOutput, calls=%fused_computation.56 | convolution fusion | flops 203489280 | bytes 4460544 | tf_op jit(solution)/shard_map/phik,phjk->phij/dot_general | solution.py:92
  206.1 3.4 fusion.31
  209.5 10.6 %fusion.7 = f32[16,64,512]{2,1,0:T(8,128)S(1)} fusion(f32[16,256,512]{2,0,1:T(8,128)S(1)} %copy-done.3, f32[16,1,64,256]{3,2,0,1:T(8,128)S(1)} %copy-done.8, f32[16,1,64,256]{3,0,1,2:T(8,128)S(1)} %copy-done.6), kind=kOutput, calls=%fused_computation.14 | convolution fusion | flops 1610874880 | bytes 12582912 | tf_op jit(solution)/shard_map/phik,phkv->phiv/dot_general | solution.py:110
  220.1 3.9 %bitcast_add_fusion = f32[16,1,64,512]{3,2,0,1:T(8,128)} fusion(f32[16,64,512]{2,1,0:T(8,128)S(1)} %fusion.31, f32[16,64,512]{2,1,0:T(8,128)S(1)} %fusion.7, f32[16,1,64,256]{3,2,0,1:T(8,128)S(1)} %copy-done.8, f32[16,1,64,256]{3,0,1,2:T(8,128)S(1)} %copy-done.6, f32[1,256,512]{2,1,0:T(8,128)S(1)} %get-tuple-element.54, ...), kind=kOutput, calls=%fused_computation.41 | convolution fusion | flops 1612447744 | bytes 8929344 | tf_op jit(solution)/shard_map/dlof,lfg->dlog/dot_general | solution.py:194
  224.0 1.8 multiply_reduce_fusion
  225.9 7.2 %fusion.25 = bf16[1024,512]{1,0:T(8,128)(2,1)} fusion(f32[16,1,64,512]{3,2,0,1:T(8,128)} %bitcast_add_fusion, f32[512]{0:T(512)S(1)} %convert_element_type.163, f32[1024]{0:T(1024)S(1)} %rsqrt.29, bf16[2048,512]{1,0:T(8,128)(2,1)} %param.25, bf16[1024,2048]{1,0:T(8,128)(2,1)} %param.18, f32[2048]{0:T(1024)S(1)} %convert_element_type.149, ...), kind=kOutput, calls=%fused_computation.45 | convolution fusion | flops 2160066560 | bytes 9455616 | tf_op jit(solution)/shard_map/dot_general | solution.py:203
  233.1 34.3 %all-gather.4.cloned.1.call-done = bf16[1408,2048]{1,0:T(8,128)(2,1)} async-done(((bf16[1408,128]{1,0:T(8,128)(2,1)}), bf16[1408,2048]{1,0:T(8,128)(2,1)}) %all-gather.4.cloned.1.call-update) | async-done | bytes 5767184 | tf_op jit(solution)/shard_map/all_gather | solution.py:163
  267.4 5.6 %convolution_convert_fusion.1 = bf16[1024,2048]{1,0:T(8,128)(2,1)} fusion(bf16[1024,512]{1,0:T(8,128)(2,1)} %fusion.25, bf16[512,2048]{1,0:T(8,128)(2,1)S(1)} %copy-done), kind=kOutput, calls=%fused_computation.37 | convolution fusion | flops 2149580800 | bytes 7340032 | tf_op jit(solution)/shard_map/dot_general | solution.py:210
  273.1 0.6 copy-done.14
  273.7 34.2 %all-reduce.3.cloned.1.call-done = bf16[1024,2048]{1,0:T(8,128)(2,1)} async-done(((bf16[1024,2048]{1,0:T(8,128)(2,1)}), bf16[1024,2048]{1,0:T(8,128)(2,1)}) %all-reduce.3.cloned.1.call-update) | async-done | bytes 4194320 | tf_op jit(solution)/shard_map/psum | solution.py:213
  307.9 5.5 %fusion = (f32[1024]{0:T(1024)S(1)}, bf16[1024,2048]{1,0:T(8,128)(2,1)S(1)}) fusion(bf16[1024,2048]{1,0:T(8,128)(2,1)} %all-reduce.3.cloned.1.call-done, bf16[1024,2048]{1,0:T(8,128)(2,1)} %param.18), kind=kLoop, calls=%fused_computation.7 | loop fusion | flops 14679040 | bytes 12587008 | tf_op jit(solution)/shard_map/reduce_sum | solution.py:45
  313.4 2.0 copy-done.9
  315.4 10.8 %fusion.34 = f32[1024,1408]{1,0:T(8,128)} fusion(bf16[2048,1408]{1,0:T(8,128)(2,1)} %all-gather.6.cloned.1.call-done, bf16[1024,2048]{1,0:T(8,128)(2,1)S(1)} %get-tuple-element.93, f32[2048]{0:T(1024)S(1)} %convert_element_type.170, f32[1024]{0:T(1024)S(1)} %add_rsqrt_fusion.1), kind=kOutput, calls=%fused_computation.57 | convolution fusion | flops 5913968640 | bytes 15740928 | tf_op jit(solution)/shard_map/dot_general | solution.py:219
  326.2 20.9 %convolution_convert_fusion = bf16[1024,2048]{1,0:T(8,128)(2,1)} fusion(bf16[1408,2048]{1,0:T(8,128)(2,1)} %all-gather.4.cloned.1.call-done, f32[1024,1408]{1,0:T(8,128)} %fusion.34, bf16[2048,1408]{1,0:T(8,128)(2,1)} %bitcast.2, bf16[1024,2048]{1,0:T(8,128)(2,1)} %copy-done.9, f32[2048]{0:T(1024)S(1)} %convert_element_type.170, f32[1024]{0:T(1024)S(1)} %add_rsqrt_fusion.1), kind=kOutput, calls=%fused_computation.36 | convolution fusion | flops 11830296576 | bytes 25702400 | tf_op jit(solution)/shard_map/dot_general | solution.py:224
  347.2 1.0 slice.93
  348.4 0.7 copy.76
  349.1 4.0 %add_convert_fusion = bf16[16,1,256,512]{3,0,2,1:T(8,128)(2,1)S(1)} fusion(f32[16,1,256,512]{3,0,2,1:T(8,128)} %copy-done.2, f32[256,512]{1,0:T(8,128)S(1)} %bitcast.121, f32[16,256]{0,1:T(8,128)S(1)} %copy.74), kind=kLoop, calls=%fused_computation.18 | loop fusion | flops 6291456 | bytes 13123584 | tf_op jit(solution)/shard_map/convert_element_type | solution.py:229
  353.1 4.5 %copy.75 = bf16[16,1,256,512]{3,2,1,0:T(8,128)(2,1)} copy(bf16[16,1,256,512]{3,0,2,1:T(8,128)(2,1)S(1)} %add_convert_fusion) | data formatting | bytes 8388608
  357.5 5.8 %reduce-scatter.2.cloned.1.call-done = bf16[512,2048]{1,0:T(8,128)(2,1)} async-done(((bf16[1024,2048]{1,0:T(8,128)(2,1)}), bf16[512,2048]{1,0:T(8,128)(2,1)}) %reduce-scatter.2.cloned.1.call-update) | async-done | bytes 2097168 | tf_op jit(solution)/shard_map/reduce_scatter | solution.py:225
  363.3 4.4 %add_convert_fusion.1 = bf16[512,2048]{1,0:T(8,128)(2,1)} fusion(bf16[512,2048]{1,0:T(8,128)(2,1)} %reduce-scatter.2.cloned.1.call-done, bf16[1024,2048]{1,0:T(8,128)(2,1)} %copy-done.9, s32[]{:T(128)S(6)} %select_n.46), kind=kLoop, calls=%fused_computation.35 | loop fusion | flops 4194304 | bytes 6291460 | tf_op jit(solution)/shard_map/convert_element_type | solution.py:228
  (76 shorter events, 1.5 us)
Async XLA Ops:
  7.2 260.2 %copy-start = (bf16[512,2048]{1,0:T(8,128)(2,1)S(1)}, bf16[512,2048]{1,0:T(8,128)(2,1)}, u32[]{:S(2)}) copy-start(bf16[512,2048]{1,0:T(8,128)(2,1)} %param.27) | copy-start | bytes 6291460
  7.2 3.3 copy-start.13
  7.2 94.6 %all-gather.8.cloned.1.call-start = ((), (), s32[]{:S(2)}) async-start(), calls=%async_computation.4 | async-start | bytes 1310720 | tf_op jit(solution)/shard_map/all_gather | solution.py:24
  7.2 3.6 copy-start.7
  10.8 13.0 %copy-start.15 = (s32[1,16]{1,0:T(1,128)S(1)}, s32[1,16]{1,0:T(1,128)}, u32[]{:S(2)}) copy-start(s32[1,16]{1,0:T(1,128)} %param.33) | copy-start | bytes 196
  10.8 13.0 %copy-start.17 = (s32[1,16]{1,0:T(1,128)S(1)}, s32[1,16]{1,0:T(1,128)}, u32[]{:S(2)}) copy-start(s32[1,16]{1,0:T(1,128)} %param.32) | copy-start | bytes 196
  10.8 13.2 %copy-start.12 = (bf16[4,1024]{1,0:T(4,128)(2,1)S(1)}, bf16[4,1024]{1,0:T(4,128)(2,1)}, u32[]{:S(2)}) copy-start(bf16[4,1024]{1,0:T(4,128)(2,1)} %param.21) | copy-start | bytes 24580
  10.8 13.2 %copy-start.18 = (bf16[2048,16]{0,1:T(8,128)(2,1)S(1)}, bf16[2048,16]{0,1:T(8,128)(2,1)}, u32[]{:S(2)}) copy-start(bf16[2048,16]{0,1:T(8,128)(2,1)} %param.22) | copy-start | bytes 196612
  10.8 13.2 %copy-start.19 = (bf16[16,256]{1,0:T(8,128)(2,1)S(1)}, bf16[16,256]{1,0:T(8,128)(2,1)}, u32[]{:S(2)}) copy-start(bf16[16,256]{1,0:T(8,128)(2,1)} %param.23) | copy-start | bytes 24580
  10.8 13.2 %copy-start.20 = (f32[256]{0:T(256)S(1)}, f32[256]{0:T(256)}, u32[]{:S(2)}) copy-start(f32[256]{0:T(256)} %param.24) | copy-start | bytes 3076
  18.1 1.3 copy-start.10
  19.4 17.3 %collective-permute-start = (bf16[3,1024]{1,0:T(4,128)(2,1)S(1)}, bf16[3,1024]{1,0:T(4,128)(2,1)S(1)}, u32[]{:S(2)}, u32[]{:S(2)}) collective-permute-start(bf16[3,1024]{1,0:T(4,128)(2,1)S(1)} %slice_bitcast_fusion.5), channel_id=1, source_target_pairs={{0,2},{2,4},{4,6},{1,3},{3,5},{5,7},{8,10},{10,12},{12,14},{9,11},... | collective-permute-start | bytes 18440 | tf_op jit(solution)/shard_map/ppermute | solution.py:18
  31.0 13.4 %copy-start.5 = (f32[16,1,64,256]{3,0,1,2:T(8,128)}, f32[16,1,64,256]{3,0,1,2:T(8,128)S(1)}, u32[]{:S(2)}) copy-start(f32[16,1,64,256]{3,0,1,2:T(8,128)S(1)} %fusion.49) | copy-start | bytes 3145732
  44.5 7.4 %copy-start.4 = (f32[16,64,1,1024]{3,1,0,2:T(8,128)}, f32[16,64,1,1024]{3,1,0,2:T(8,128)S(1)}, u32[]{:S(2)}) copy-start(f32[16,64,1,1024]{3,1,0,2:T(8,128)S(1)} %fusion.15) | copy-start | bytes 12582916
  51.9 19.7 %copy-start.11 = (bf16[128,1408]{1,0:T(8,128)(2,1)S(1)}, bf16[128,1408]{1,0:T(8,128)(2,1)}, u32[]{:S(2)}) copy-start(bf16[128,1408]{1,0:T(8,128)(2,1)} %param.30) | copy-start | bytes 1081348
  65.5 3.2 copy-start.2
  70.1 131.2 %all-gather.6.cloned.1.call-start = ((), (), s32[]{:S(2)}) async-start(), calls=%async_computation.3 | async-start | bytes 6127616 | tf_op jit(solution)/shard_map/all_gather | solution.py:153
  70.9 196.6 %all-gather.4.cloned.1.call-start = ((), (), s32[]{:S(2)}) async-start(), calls=%async_computation.2 | async-start | bytes 6127616 | tf_op jit(solution)/shard_map/all_gather | solution.py:163
  74.6 7.8 %copy-start.16 = (bf16[512]{0:T(512)(128)(2,1)S(1)}, bf16[512]{0:T(512)(128)(2,1)}, u32[]{:S(2)}) copy-start(bf16[512]{0:T(512)(128)(2,1)} %param.26) | copy-start | bytes 3076
  74.6 149.3 %all-to-all-start = ((bf16[16,128,1408]{2,1,0:T(8,128)(2,1)}), bf16[16,128,1408]{2,1,0:T(8,128)(2,1)}, u32[]{:S(2)}, u32[]{:S(2)}) async-start(bf16[16,128,1408]{2,1,0:T(8,128)(2,1)} %stack.2), calls=%async_computation | async-start | bytes 11534336 | tf_op jit(solution)/shard_map/all_to_all | solution.py:155
  81.6 226.3 %all-reduce.3.cloned.1.call-start = ((), (), s32[]{:S(2)}) async-start(), calls=%async_computation.5 | async-start | bytes 8388608 | tf_op jit(solution)/shard_map/psum | solution.py:213
  201.3 8.2 %copy-start.3 = (f32[16,256,512]{2,0,1:T(8,128)S(1)}, f32[16,256,512]{2,0,1:T(8,128)}, u32[]{:S(2)}) copy-start(f32[16,256,512]{2,0,1:T(8,128)} %multiply_bitcast_fusion) | copy-start | bytes 25165828
  201.3 8.2 %copy-start.6 = (f32[16,1,64,256]{3,0,1,2:T(8,128)S(1)}, f32[16,1,64,256]{3,0,1,2:T(8,128)}, u32[]{:S(2)}) copy-start(f32[16,1,64,256]{3,0,1,2:T(8,128)} %copy-done.5) | copy-start | bytes 3145732
  201.3 8.2 %copy-start.8 = (f32[16,1,64,256]{3,2,0,1:T(8,128)S(1)}, f32[16,1,64,256]{3,2,0,1:T(8,128)}, u32[]{:S(2)}) copy-start(f32[16,1,64,256]{3,2,0,1:T(8,128)} %multiply_bitcast_fusion.1) | copy-start | bytes 3145732
  273.0 0.7 copy-start.14
  273.0 90.3 %reduce-scatter.2.cloned.1.call-start = ((), (), s32[]{:S(2)}) async-start(), calls=%async_computation.6 | async-start | bytes 6291456 | tf_op jit(solution)/shard_map/reduce_scatter | solution.py:225
  313.4 2.1 copy-start.9
  353.0 14.7 %copy-start.1 = (bf16[512,2048]{1,0:T(8,128)(2,1)S(1)}, bf16[512,2048]{1,0:T(8,128)(2,1)}, u32[]{:S(2)}) copy-start(bf16[512,2048]{1,0:T(8,128)(2,1)} %param.27) | copy-start | bytes 6291460
Sparse Core Ops, SparseCore 0:
  70.2 25.4 all-gather.7
  97.9 103.3 all-gather.5
  203.4 63.9 all-gather.3
  273.1 34.7 all-reduce.2
  347.3 15.9 reduce-scatter.1
